TPU v7x, 32 devices: a whole 2x2x4 slice. The times are simulated.
32 devices in a mesh: shards: 4 (over x, core), context: 2 (over y), tensor: 4 (over z).
Axes of the slice: x: 2, y: 2, z: 4, core: 2. Of those that a mesh axis runs over, the one named last changes fastest.
Arguments:
- tokens: bfloat16 [8192, 1280], P(('shards', 'context')), may hold values from -6 to 6
- cotangent: bfloat16 [8192, 1280], P(('shards', 'context')), may hold values from -6 to 6
- segments: int32 [8192], P(('shards', 'context')), may hold values from 0 to 1024, as said below
- positions: int32 [8192], P(('shards', 'context')), may hold values from 0 to 1279, as said below
- w_query: bfloat16 [1280, 1280], P('shards', 'tensor'), may hold values from -0.15625 to 0.15625
- w_key: bfloat16 [1280, 1280], P('shards', 'tensor'), may hold values from -0.15625 to 0.15625
- w_value: bfloat16 [1280, 1280], P('shards', 'tensor'), may hold values from -0.15625 to 0.15625
- w_output: bfloat16 [1280, 1280], P('tensor', 'shards'), may hold values from -0.15625 to 0.15625
- w_up: bfloat16 [1280, 5120], P('shards', 'tensor'), may hold values from -0.15625 to 0.15625
- w_gate: bfloat16 [1280, 5120], P('shards', 'tensor'), may hold values from -0.15625 to 0.15625
- w_down: bfloat16 [5120, 1280], P('tensor', 'shards'), may hold values from -0.078125 to 0.078125
- scale_qk: float32 [1280], P('tensor'), may hold values from 1 to 1.6
- alpha_attn: float32 [1280], replicated, may hold values from 0.15 to 0.6
- alpha_mlp: float32 [1280], replicated, may hold values from 0.15 to 0.6
- scale_up: float32 [5120], P('tensor'), may hold values from 0.25 to 1.75
- scale_gate: float32 [5120], P('tensor'), may hold values from 0.25 to 1.75
Outputs:
- block_out: bfloat16 [8192, 1280], P(('shards', 'context'))
- grad_tokens: bfloat16 [8192, 1280], P(('shards', 'context'))
- grad_query: float32 [1280, 1280], P('shards', 'tensor')
- grad_key: float32 [1280, 1280], P('shards', 'tensor')
- grad_value: float32 [1280, 1280], P('shards', 'tensor')
- grad_output: float32 [1280, 1280], P('tensor', 'shards')
- grad_up: float32 [1280, 5120], P('shards', 'tensor')
- grad_gate: float32 [1280, 5120], P('shards', 'tensor')
- grad_down: float32 [5120, 1280], P('tensor', 'shards')
- grad_scale_qk: float32 [1280], P('tensor')
- grad_alpha_attn: float32 [1280], replicated
- grad_alpha_mlp: float32 [1280], replicated
- grad_scale_up: float32 [5120], P('tensor')
- grad_scale_gate: float32 [5120], P('tensor')
Inputs may be any that keep to these rules, and one draw needn't show every extreme that they name: `segments`: each run of 1024 tokens in order (one device of shards and context) holds first 512 prompt tokens (id 0), the prompt's tokens lying in order over the group, then 512 slots filled with whole continuations of 1 to 256 tokens each, one of exactly 256; a continuation's tokens are consecutive and its id is shared by no other continuation of the group. `positions`: A prompt token's position is its index in the group's prompt; a continuation token's is 1024 plus its offset in its continuation.
All inputs are finite; a program needn't handle non-finite values.
Results may differ from a plain program's by a relative error of at most 0.02.
Values may be sent and summed in bfloat16 or wider, within the bound.
No kernel may reach another device: no remote copies, remote signals or barrier semaphores. Data moves between devices by JAX's collectives and lax.ppermute only.
A program may use at most 192 MiB of HBM per device.

v0:
```python
import math
import jax
import jax.numpy as jnp
from jax import lax
from jax.sharding import PartitionSpec as P

HD = 64
CONT_DEV = 2
CONT_LEN = 256
EPSILON = 1e-06
MASKED = -1e30


def renorm(vector):
    return vector * lax.rsqrt(jnp.mean(vector * vector, axis=-1, keepdims=True) + EPSILON)


def rotate(values, cosine_table, sine_table):
    half_size = values.shape[-1] // 2
    first_half = values[..., :half_size]
    second_half = values[..., half_size:]
    return jnp.concatenate(
        [
            first_half * cosine_table - second_half * sine_table,
            second_half * cosine_table + first_half * sine_table,
        ],
        axis=-1,
    )


def head_norm(raw_heads, cosine_table, sine_table, factor):
    turned = rotate(raw_heads, cosine_table[:, None, :], sine_table[:, None, :])
    return factor * turned * lax.rsqrt(jnp.sum(turned * turned, axis=-1, keepdims=True) + EPSILON)


def residual_step(hidden, branch, alpha):
    return renorm(hidden + alpha * (renorm(branch) - hidden))


def swiglu(up_proj, gate_proj, scale_up, scale_gate):
    return scale_up * up_proj * jax.nn.silu(scale_gate * gate_proj)


def phase_tables(positions, head_size):
    half_size = head_size // 2
    frequency = 10000.0 ** (-(jnp.arange(half_size, dtype=jnp.float32) * 2.0 / head_size))
    phases = positions.astype(jnp.float32)[:, None] * frequency[None, :]
    return (jnp.cos(phases), jnp.sin(phases))


def outer_sum(left, right):
    return lax.dot_general(
        left, right, (((0,), (0,)), ((), ())), preferred_element_type=jnp.float32
    )


def back_product(gradient, weight):
    return lax.dot_general(
        gradient, weight, (((1,), (1,)), ((), ())), preferred_element_type=jnp.float32
    )


def to_heads(flat, head_size):
    return jnp.swapaxes(flat.reshape(flat.shape[0], -1, head_size), 0, 1)


def from_heads(stacked):
    return jnp.swapaxes(stacked, 0, 1).reshape(stacked.shape[1], -1)


def on_device(
    tokens,
    cotangent,
    segments,
    positions,
    w_query,
    w_key,
    w_value,
    w_output,
    w_up,
    w_gate,
    w_down,
    scale_qk,
    alpha_attn,
    alpha_mlp,
    scale_up,
    scale_gate,
):
    full_query, full_key, full_value, full_output, full_up, full_gate, full_down = (
        lax.all_gather(w_query, "shards", axis=0, tiled=True),
        lax.all_gather(w_key, "shards", axis=0, tiled=True),
        lax.all_gather(w_value, "shards", axis=0, tiled=True),
        lax.all_gather(w_output, "shards", axis=1, tiled=True),
        lax.all_gather(w_up, "shards", axis=0, tiled=True),
        lax.all_gather(w_gate, "shards", axis=0, tiled=True),
        lax.all_gather(w_down, "shards", axis=1, tiled=True),
    )
    row_count = tokens.shape[0]
    prompt_rows = row_count - CONT_DEV * CONT_LEN
    heads_local = scale_qk.shape[0] // HD
    multiplier = math.sqrt(HD)
    factor = scale_qk.reshape(heads_local, HD)
    cosine_table, sine_table = phase_tables(positions, HD)

    def normalize(raw_heads, factor_heads):
        return head_norm(raw_heads, cosine_table, sine_table, factor_heads)

    query_raw = jnp.dot(tokens, full_query, preferred_element_type=jnp.float32).reshape(
        row_count, heads_local, HD
    )
    key_raw = jnp.dot(tokens, full_key, preferred_element_type=jnp.float32).reshape(
        row_count, heads_local, HD
    )
    value_low = jnp.dot(tokens, full_value, preferred_element_type=jnp.float32).astype(jnp.bfloat16)
    query_normed, query_back = jax.vjp(normalize, query_raw, factor)
    key_normed, key_back = jax.vjp(normalize, key_raw, factor)
    query_low = query_normed.astype(jnp.bfloat16).reshape(row_count, -1)
    key_low = key_normed.astype(jnp.bfloat16).reshape(row_count, -1)
    prompt_keys, prompt_values = (
        lax.all_gather(key_low[:prompt_rows], "context", axis=0, tiled=True),
        lax.all_gather(value_low[:prompt_rows], "context", axis=0, tiled=True),
    )
    prompt_total = prompt_keys.shape[0]
    key_positions = jnp.concatenate(
        [jnp.arange(prompt_total, dtype=jnp.int32), positions[prompt_rows:]]
    )
    key_segments = jnp.concatenate([jnp.zeros((prompt_total,), jnp.int32), segments[prompt_rows:]])
    allowed = (key_positions[None, :] <= positions[:, None]) & (
        (key_segments[None, :] == 0) | (key_segments[None, :] == segments[:, None])
    )
    key_heads = to_heads(jnp.concatenate([prompt_keys, key_low[prompt_rows:]], axis=0), HD)
    value_heads = to_heads(jnp.concatenate([prompt_values, value_low[prompt_rows:]], axis=0), HD)
    key_heads, value_heads = (key_heads, value_heads)
    query_heads = to_heads(query_low, HD)

    def masked_scores(query_head, key_head):
        scores = multiplier * jnp.einsum(
            "qd,kd->qk", query_head, key_head, preferred_element_type=jnp.float32
        )
        return jnp.where(allowed, scores, MASKED)

    def attend_head(operands):
        query_head, key_head, value_head = operands
        scores = masked_scores(query_head, key_head)
        row_peak = jnp.max(scores, axis=1, keepdims=True)
        weights = jnp.exp(scores - row_peak)
        row_total = jnp.sum(weights, axis=1, keepdims=True)
        softmax_low = (weights / row_total).astype(jnp.bfloat16)
        head_out = jnp.dot(softmax_low, value_head, preferred_element_type=jnp.float32).astype(
            jnp.bfloat16
        )
        return (head_out, (row_peak + jnp.log(row_total))[:, 0])

    mixed_heads, log_totals = lax.map(attend_head, (query_heads, key_heads, value_heads))
    mixed_low = from_heads(mixed_heads)
    attn_terms = jnp.dot(mixed_low, full_output, preferred_element_type=jnp.float32)
    attn_out = lax.psum(attn_terms, "tensor")
    after_attn, attn_back = jax.vjp(residual_step, tokens.astype(jnp.float32), attn_out, alpha_attn)
    after_low = after_attn.astype(jnp.bfloat16)
    up_proj = jnp.dot(after_low, full_up, preferred_element_type=jnp.float32)
    gate_proj = jnp.dot(after_low, full_gate, preferred_element_type=jnp.float32)
    inner, swiglu_back = jax.vjp(swiglu, up_proj, gate_proj, scale_up, scale_gate)
    inner_low = inner.astype(jnp.bfloat16)
    merged_terms = jnp.dot(inner_low, full_down, preferred_element_type=jnp.float32)
    merged = lax.psum(merged_terms, "tensor")
    block_whole, out_back = jax.vjp(residual_step, after_attn, merged, alpha_mlp)
    block_low = block_whole.astype(jnp.bfloat16)
    grad_after, grad_merged, grad_alpha_mlp = out_back(cotangent.astype(jnp.float32))
    merged_grad_low = grad_merged.astype(jnp.bfloat16)
    grad_down = outer_sum(inner_low, merged_grad_low)
    grad_up_proj, grad_gate_proj, grad_scale_up, grad_scale_gate = swiglu_back(
        back_product(merged_grad_low, full_down)
    )
    up_grad_low = grad_up_proj.astype(jnp.bfloat16)
    gate_grad_low = grad_gate_proj.astype(jnp.bfloat16)
    grad_up = outer_sum(after_low, up_grad_low)
    grad_gate = outer_sum(after_low, gate_grad_low)
    input_terms = back_product(up_grad_low, full_up) + back_product(gate_grad_low, full_gate)
    grad_after = grad_after + lax.psum(input_terms, "tensor")
    grad_tokens_direct, grad_attn, grad_alpha_attn = attn_back(grad_after)
    attn_grad_low = grad_attn.astype(jnp.bfloat16)
    grad_output = outer_sum(mixed_low, attn_grad_low)
    grad_mixed_heads = to_heads(back_product(attn_grad_low, full_output).astype(jnp.bfloat16), HD)
    back_keys, back_values = (key_heads, value_heads)

    def head_backward(operands):
        query_head, key_head, value_head, grad_head, log_total = operands
        softmax_full = jnp.exp(masked_scores(query_head, key_head) - log_total[:, None])
        grad_softmax = jnp.einsum(
            "qd,kd->qk", grad_head, value_head, preferred_element_type=jnp.float32
        )
        weighted = jnp.sum(softmax_full * grad_softmax, axis=1, keepdims=True)
        grad_scores = (softmax_full * (grad_softmax - weighted)).astype(jnp.bfloat16)
        grad_query_head = multiplier * jnp.dot(
            grad_scores, key_head, preferred_element_type=jnp.float32
        )
        grad_key_head = multiplier * outer_sum(grad_scores, query_head)
        grad_value_head = outer_sum(softmax_full.astype(jnp.bfloat16), grad_head)
        return (grad_query_head, grad_key_head, grad_value_head)

    grad_query_heads, grad_key_heads, grad_value_heads = lax.map(
        head_backward, (query_heads, back_keys, back_values, grad_mixed_heads, log_totals)
    )
    grad_key_flat = from_heads(grad_key_heads)
    grad_value_flat = from_heads(grad_value_heads)
    prompt_grad_keys, prompt_grad_values = (
        lax.psum_scatter(
            grad_key_flat[:prompt_total].astype(jnp.bfloat16),
            "context",
            scatter_dimension=0,
            tiled=True,
        ).astype(jnp.float32),
        lax.psum_scatter(
            grad_value_flat[:prompt_total].astype(jnp.bfloat16),
            "context",
            scatter_dimension=0,
            tiled=True,
        ).astype(jnp.float32),
    )
    grad_key_rows = jnp.concatenate([prompt_grad_keys, grad_key_flat[prompt_total:]], axis=0)
    grad_value_rows = jnp.concatenate([prompt_grad_values, grad_value_flat[prompt_total:]], axis=0)
    grad_query_raw, grad_factor_query = query_back(
        from_heads(grad_query_heads).reshape(row_count, heads_local, HD)
    )
    grad_key_raw, grad_factor_key = key_back(grad_key_rows.reshape(row_count, heads_local, HD))
    query_grad_low = grad_query_raw.reshape(row_count, -1).astype(jnp.bfloat16)
    key_grad_low = grad_key_raw.reshape(row_count, -1).astype(jnp.bfloat16)
    value_grad_low = grad_value_rows.astype(jnp.bfloat16)
    grad_query = outer_sum(tokens, query_grad_low)
    grad_key = outer_sum(tokens, key_grad_low)
    grad_value = outer_sum(tokens, value_grad_low)
    token_terms = (
        back_product(query_grad_low, full_query)
        + back_product(key_grad_low, full_key)
        + back_product(value_grad_low, full_value)
    )
    grad_tokens = (
        grad_tokens_direct
        + lax.psum(token_terms.astype(jnp.bfloat16), "tensor").astype(jnp.float32)
    ).astype(jnp.bfloat16)
    grad_scale_qk = (grad_factor_query + grad_factor_key).reshape(-1)
    shard_query, shard_key, shard_value, shard_output, shard_up, shard_gate, shard_down = (
        lax.psum_scatter(
            grad_query.astype(jnp.bfloat16), "shards", scatter_dimension=0, tiled=True
        ).astype(jnp.float32),
        lax.psum_scatter(
            grad_key.astype(jnp.bfloat16), "shards", scatter_dimension=0, tiled=True
        ).astype(jnp.float32),
        lax.psum_scatter(
            grad_value.astype(jnp.bfloat16), "shards", scatter_dimension=0, tiled=True
        ).astype(jnp.float32),
        lax.psum_scatter(
            grad_output.astype(jnp.bfloat16), "shards", scatter_dimension=1, tiled=True
        ).astype(jnp.float32),
        lax.psum_scatter(
            grad_up.astype(jnp.bfloat16), "shards", scatter_dimension=0, tiled=True
        ).astype(jnp.float32),
        lax.psum_scatter(
            grad_gate.astype(jnp.bfloat16), "shards", scatter_dimension=0, tiled=True
        ).astype(jnp.float32),
        lax.psum_scatter(
            grad_down.astype(jnp.bfloat16), "shards", scatter_dimension=1, tiled=True
        ).astype(jnp.float32),
    )
    part_query, part_key, part_value, part_output, part_up, part_gate, part_down = (
        lax.psum_scatter(
            shard_query.astype(jnp.bfloat16), "context", scatter_dimension=0, tiled=True
        ).astype(jnp.float32),
        lax.psum_scatter(
            shard_key.astype(jnp.bfloat16), "context", scatter_dimension=0, tiled=True
        ).astype(jnp.float32),
        lax.psum_scatter(
            shard_value.astype(jnp.bfloat16), "context", scatter_dimension=0, tiled=True
        ).astype(jnp.float32),
        lax.psum_scatter(
            shard_output.astype(jnp.bfloat16), "context", scatter_dimension=1, tiled=True
        ).astype(jnp.float32),
        lax.psum_scatter(
            shard_up.astype(jnp.bfloat16), "context", scatter_dimension=0, tiled=True
        ).astype(jnp.float32),
        lax.psum_scatter(
            shard_gate.astype(jnp.bfloat16), "context", scatter_dimension=0, tiled=True
        ).astype(jnp.float32),
        lax.psum_scatter(
            shard_down.astype(jnp.bfloat16), "context", scatter_dimension=1, tiled=True
        ).astype(jnp.float32),
    )
    sum_query, sum_key, sum_value, sum_output, sum_up, sum_gate, sum_down = (
        lax.all_gather(part_query.astype(jnp.bfloat16), "context", axis=0, tiled=True).astype(
            part_query.dtype
        ),
        lax.all_gather(part_key.astype(jnp.bfloat16), "context", axis=0, tiled=True).astype(
            part_key.dtype
        ),
        lax.all_gather(part_value.astype(jnp.bfloat16), "context", axis=0, tiled=True).astype(
            part_value.dtype
        ),
        lax.all_gather(part_output.astype(jnp.bfloat16), "context", axis=1, tiled=True).astype(
            part_output.dtype
        ),
        lax.all_gather(part_up.astype(jnp.bfloat16), "context", axis=0, tiled=True).astype(
            part_up.dtype
        ),
        lax.all_gather(part_gate.astype(jnp.bfloat16), "context", axis=0, tiled=True).astype(
            part_gate.dtype
        ),
        lax.all_gather(part_down.astype(jnp.bfloat16), "context", axis=1, tiled=True).astype(
            part_down.dtype
        ),
    )
    total_scale_qk, total_alpha_attn, total_alpha_mlp, total_scale_up, total_scale_gate = lax.psum(
        (grad_scale_qk, grad_alpha_attn, grad_alpha_mlp, grad_scale_up, grad_scale_gate),
        ("shards", "context"),
    )
    return (
        block_low,
        grad_tokens,
        sum_query,
        sum_key,
        sum_value,
        sum_output,
        sum_up,
        sum_gate,
        sum_down,
        total_scale_qk,
        total_alpha_attn,
        total_alpha_mlp,
        total_scale_up,
        total_scale_gate,
    )


def solution(mesh):
    in_specs = (
        P(("shards", "context"), None),
        P(("shards", "context"), None),
        P(("shards", "context")),
        P(("shards", "context")),
        P("shards", "tensor"),
        P("shards", "tensor"),
        P("shards", "tensor"),
        P("tensor", "shards"),
        P("shards", "tensor"),
        P("shards", "tensor"),
        P("tensor", "shards"),
        P("tensor"),
        P(),
        P(),
        P("tensor"),
        P("tensor"),
    )
    out_specs = (
        P(("shards", "context"), None),
        P(("shards", "context"), None),
        P("shards", "tensor"),
        P("shards", "tensor"),
        P("shards", "tensor"),
        P("tensor", "shards"),
        P("shards", "tensor"),
        P("shards", "tensor"),
        P("tensor", "shards"),
        P("tensor"),
        P(),
        P(),
        P("tensor"),
        P("tensor"),
    )
    return jax.shard_map(
        on_device, mesh=mesh, in_specs=in_specs, out_specs=out_specs, check_vma=False
    )
```

profile of v0, /device:TPU:0, one launch (start us, length us, event | category | flops | bytes accessed | tf_op | source)
XLA Modules:
  0.0 1299.2 jit_solution(2730937836505166477)
XLA Ops:
  11.3 11.3 all_gather.48
  22.7 10.1 all_gather.49
  32.8 3.2 fusion.70
  39.9 10.6 all_gather.50
  55.8 9.5 all_gather.51
  66.5 10.8 all_gather.52
  81.5 57.1 %while.28 = (s32[]{:T(128)}, bf16[5,1024,64]{1,2,0:T(8,128)(2,1)S(1)}, f32[5,1024]{1,0:T(8,128)S(1)}, bf16[5,1024,64]{2,1,0:T(8,128)(2,1)}, bf16[5,1536,64]{2,1,...) while((s32[]{:T(128)}, ...), condition=%wide.region_5.6_spmd.clone, body=%wide.region_2.5_spmd.clone.sunk | while | flops 421592064 | bytes 45289628 | solution.py:154
  81.6 3.4 fusion.135
  88.8 4.2 fusion.137
  93.0 3.4 fusion.135
  100.2 4.2 fusion.137
  104.4 3.4 fusion.135
  111.6 4.2 fusion.137
  115.8 3.4 fusion.135
  123.0 4.2 fusion.137
  127.2 3.4 fusion.135
  134.4 4.2 fusion.137
  140.0 9.3 all_gather.53
  150.3 3.9 fusion.72
  156.1 188.1 %all-reduce.11.cloned.1.call-done = f32[1024,1280]{1,0:T(8,128)} async-done(((f32[1024,1280]{1,0:T(8,128)}), f32[1024,1280]{1,0:T(8,128)}) %all-reduce.11.cloned.1.call-update) | async-done | bytes 5242896 | tf_op jit(solution)/shard_map/psum | solution.py:157
  352.4 8.1 fusion.73
  360.6 8.7 multiply_convert_fusion.4
  369.3 8.7 fusion.74
  378.4 187.5 %all-reduce.13.cloned.1.call-done = f32[1024,1280]{1,0:T(8,128)} async-done(((f32[1024,1280]{1,0:T(8,128)}), f32[1024,1280]{1,0:T(8,128)}) %all-reduce.13.cloned.1.call-update) | async-done | bytes 5242896 | tf_op jit(solution)/shard_map/psum | solution.py:165
  570.0 4.7 fusion.49
  574.8 3.1 multiply_reduce_fusion.7
  581.1 9.5 multiply_reduce_fusion.1
  590.7 3.6 fusion.75
  595.0 5.5 convolution_add_fusion
  600.8 187.8 %all-reduce.15.cloned.1.call-done = f32[1024,1280]{1,0:T(8,128)} async-done(((f32[1024,1280]{1,0:T(8,128)}), f32[1024,1280]{1,0:T(8,128)}) %all-reduce.15.cloned.1.call-update) | async-done | bytes 5242896 | tf_op jit(solution)/shard_map/psum | solution.py:179
  788.5 9.5 multiply_reduce_fusion.3
  798.1 11.6 multiply_reduce_fusion.4
  814.4 68.5 %while.29 = (s32[]{:T(128)}, f32[5,1024,64]{1,2,0:T(8,128)}, f32[5,1536,64]{1,2,0:T(8,128)}, bf16[5,1536,64]{1,2,0:T(8,128)(2,1)}, bf16[5,1024,64]{2,1,0:T(8,128...) while((s32[]{:T(128)}, f32[5,1024,64]{1,2,0:T(8,128)}, ...), condition=%wide.region_19.20_spmd.clone, body=%wide.region_17.19_spmd.clone.sunk | while | flops 1027243008 | bytes 50515088 | solution.py:201
  816.5 4.5 multiply_reduce_fusion.18
  830.2 4.5 multiply_reduce_fusion.18
  843.9 4.5 multiply_reduce_fusion.18
  857.5 4.5 multiply_reduce_fusion.18
  871.3 4.5 multiply_reduce_fusion.18
  887.7 3.8 convolution_convert_fusion.3
  893.8 6.8 convolution_convert_fusion
  902.3 6.7 convolution_convert_fusion.2
  909.2 7.5 convolution_convert_fusion.1
  921.6 4.0 fusion.57
  945.7 40.9 %reduce-scatter.45.cloned.1.call-done = bf16[1280,320]{0,1:T(8,128)(2,1)} async-done(((bf16[1280,1280]{0,1:T(8,128)(2,1)}), bf16[1280,320]{0,1:T(8,128)(2,1)}) %reduce-scatter.45.cloned.1.call-update) | async-done | bytes 819216 | tf_op jit(solution)/shard_map/reduce_scatter | solution.py:261
  986.7 40.9 %reduce-scatter.37.cloned.1.call-done = bf16[320,1280]{1,0:T(8,128)(2,1)} async-done(((bf16[1280,1280]{1,0:T(8,128)(2,1)}), bf16[320,1280]{1,0:T(8,128)(2,1)}) %reduce-scatter.37.cloned.1.call-update) | async-done | bytes 819216 | tf_op jit(solution)/shard_map/reduce_scatter | solution.py:255
  1027.8 40.9 %reduce-scatter.41.cloned.1.call-done = bf16[320,1280]{1,0:T(8,128)(2,1)} async-done(((bf16[1280,1280]{1,0:T(8,128)(2,1)}), bf16[320,1280]{1,0:T(8,128)(2,1)}) %reduce-scatter.41.cloned.1.call-update) | async-done | bytes 819216 | tf_op jit(solution)/shard_map/reduce_scatter | solution.py:258
  1068.8 27.5 %reduce-scatter.57.cloned.1.call-done = bf16[320,320]{1,0:T(8,128)(2,1)} async-done(((bf16[1280,320]{1,0:T(8,128)(2,1)}), bf16[320,320]{1,0:T(8,128)(2,1)}) %reduce-scatter.57.cloned.1.call-update) | async-done | bytes 204816
  1096.3 27.3 %reduce-scatter.53.cloned.1.call-done = bf16[320,320]{1,0:T(8,128)(2,1)} async-done(((bf16[1280,320]{1,0:T(8,128)(2,1)}), bf16[320,320]{1,0:T(8,128)(2,1)}) %reduce-scatter.53.cloned.1.call-update) | async-done | bytes 204816
  1123.7 3.9 fusion.77
  1127.7 3.8 fusion.76
  1131.5 19.6 %reduce-scatter.49.cloned.1.call-done = bf16[320,320]{1,0:T(8,128)(2,1)} async-done(((bf16[1280,320]{1,0:T(8,128)(2,1)}), bf16[320,320]{1,0:T(8,128)(2,1)}) %reduce-scatter.49.cloned.1.call-update) | async-done | bytes 204816
  1151.3 7.1 add_convert_fusion.1
  1158.5 26.4 %all-reduce.5 = (f32[320]{0:T(512)}, f32[1280]{0:T(1024)}, f32[1280]{0:T(1024)}, f32[1280]{0:T(1024)}, f32[1280]{0:T(1024)}) all-reduce(f32[320]{0:T(512)S(1)} %add.196, f32[1280]{0:T(1024)S(1)} %copy-done.58, f32[1280]{0:T(1024)S(1)} %copy-done.57, ...), channel_id=1, replica_groups=mesh['shards'=4,'context'=2,'tensor'=4] {'shards','context'}, use_global_device_ids=true, to_apply=%region_41.42 | all-reduce | flops 5440 | bytes 43520 | tf_op jit(solution)/shard_map/psum | solution.py:311
  1184.9 5.7 all_gather.60
  1191.6 19.3 %all_gather.63 = bf16[1280,320]{0,1:T(8,128)(2,1)S(1)} all-gather(bf16[1280,160]{0,1:T(8,128)(2,1)} %reduce-scatter.47.cloned.1.call-done), channel_id=1, replica_groups=mesh['shards'=4,'context'=2,'tensor'=4] {'context'}, dimensions={1}, use_global_device_ids=true | all-gather | bytes 1228800 | tf_op jit(solution)/shard_map/all_gather | solution.py:307
  1212.5 13.6 %all_gather.61 = bf16[320,1280]{1,0:T(8,128)(2,1)S(1)} all-gather(bf16[160,1280]{1,0:T(8,128)(2,1)} %reduce-scatter.39.cloned.1.call-done), channel_id=1, replica_groups=mesh['shards'=4,'context'=2,'tensor'=4] {'context'}, dimensions={0}, use_global_device_ids=true | all-gather | bytes 1228800 | tf_op jit(solution)/shard_map/all_gather | solution.py:301
  1227.3 7.2 reduce-scatter.43.cloned.1.call-done
  1234.5 13.6 %all_gather.62 = bf16[320,1280]{1,0:T(8,128)(2,1)S(1)} all-gather(bf16[160,1280]{1,0:T(8,128)(2,1)} %reduce-scatter.43.cloned.1.call-done), channel_id=1, replica_groups=mesh['shards'=4,'context'=2,'tensor'=4] {'context'}, dimensions={0}, use_global_device_ids=true | all-gather | bytes 1228800 | tf_op jit(solution)/shard_map/all_gather | solution.py:304
  1250.1 5.9 all_gather.59
  1256.9 8.7 reduce-scatter.55.cloned.1.call-done
  1265.5 5.7 all_gather.58
  1272.1 7.1 reduce-scatter.51.cloned.1.call-done
  1279.1 5.7 all_gather.57
  1285.7 5.7 add_convert_fusion
  (343 shorter events, 150.5 us)
Async XLA Ops:
  8.0 336.2 %all-reduce.11.cloned.1.call-start = ((), (), s32[]{:S(2)}) async-start(), calls=%async_computation.16 | async-start | bytes 10485760 | tf_op jit(solution)/shard_map/psum | solution.py:157
  22.7 13.3 %copy-start.24 = (bf16[1280,320]{1,0:T(8,128)(2,1)}, bf16[1280,320]{1,0:T(8,128)(2,1)S(1)}, u32[]{:S(2)}) copy-start(bf16[1280,320]{1,0:T(8,128)(2,1)S(1)} %all_gather.48) | copy-start | bytes 2457604
  22.7 13.3 %copy-start.15 = (bf16[1024,1280]{1,0:T(8,128)(2,1)S(1)}, bf16[1024,1280]{1,0:T(8,128)(2,1)}, u32[]{:S(2)}) copy-start(bf16[1024,1280]{1,0:T(8,128)(2,1)} %param.20) | copy-start | bytes 7864324
  38.5 13.1 %copy-start.43 = (f32[1024,5]{0,1:T(8,128)}, f32[1024,5]{0,1:T(8,128)S(1)}, u32[]{:S(2)}) copy-start(f32[1024,5]{0,1:T(8,128)S(1)} %add_rsqrt_fusion) | copy-start | bytes 61444
  39.4 12.1 copy-start.45
  39.5 12.1 copy-start.55
  51.6 13.7 %copy-start.16 = (bf16[1024,1280]{1,0:T(8,128)(2,1)S(1)}, bf16[1024,1280]{1,0:T(8,128)(2,1)}, u32[]{:S(2)}) copy-start(bf16[1024,1280]{1,0:T(8,128)(2,1)} %param.20) | copy-start | bytes 7864324
  66.4 15.1 %copy-start.35 = (bf16[5,1024,64]{1,2,0:T(8,128)(2,1)S(1)}, bf16[5,1024,64]{1,2,0:T(8,128)(2,1)}, u32[]{:S(2)}) copy-start(bf16[5,1024,64]{1,2,0:T(8,128)(2,1)} %custom-call) | copy-start | bytes 1966084
  66.4 15.1 %copy-start.59 = (s32[1024]{0:T(1024)S(1)}, s32[1024]{0:T(1024)}, u32[]{:S(2)}) copy-start(s32[1024]{0:T(1024)} %param.23) | copy-start | bytes 12292
  66.5 15.1 %copy-start.64 = (s32[1024]{0:T(1024)S(1)}, s32[1024]{0:T(1024)}, u32[]{:S(2)}) copy-start(s32[1024]{0:T(1024)} %param.22) | copy-start | bytes 12292
  138.6 15.6 %copy-start.36 = (bf16[5,1024,64]{1,2,0:T(8,128)(2,1)}, bf16[5,1024,64]{1,2,0:T(8,128)(2,1)S(1)}, u32[]{:S(2)}) copy-start(bf16[5,1024,64]{1,2,0:T(8,128)(2,1)S(1)} %get-tuple-element.106) | copy-start | bytes 1966084
  154.3 198.1 %all-gather.6.cloned.1.call-start = ((), (), s32[]{:S(2)}) async-start(), calls=%async_computation.18 | async-start | bytes 4096000 | tf_op jit(solution)/shard_map/all_gather | solution.py:95
  154.9 192.4 %copy-start.53 = (f32[1280]{0:T(1024)S(1)}, f32[1280]{0:T(1024)}, u32[]{:S(2)}) copy-start(f32[1280]{0:T(1024)} %param.32) | copy-start | bytes 15364
  154.9 205.7 %all-gather.4.cloned.1.call-start = ((), (), s32[]{:S(2)}) async-start(), calls=%async_computation.17 | async-start | bytes 4096000 | tf_op jit(solution)/shard_map/all_gather | solution.py:94
  155.5 213.8 %all-gather.8.cloned.1.call-start = ((), (), s32[]{:S(2)}) async-start(), calls=%async_computation.19 | async-start | bytes 4096000 | tf_op jit(solution)/shard_map/all_gather | solution.py:96
  156.0 410.0 %all-reduce.13.cloned.1.call-start = ((), (), s32[]{:S(2)}) async-start(), calls=%async_computation.20 | async-start | bytes 10485760 | tf_op jit(solution)/shard_map/psum | solution.py:165
  352.3 8.2 copy-start.30
  352.4 8.2 copy-start.69
  352.4 8.2 copy-start.70
  378.0 191.1 %copy-start.4 = (bf16[1024,1280]{1,0:T(8,128)(2,1)S(1)}, bf16[1024,1280]{1,0:T(8,128)(2,1)}, u32[]{:S(2)}) copy-start(bf16[1024,1280]{1,0:T(8,128)(2,1)} %param.21) | copy-start | bytes 7864324
  378.0 191.1 %copy-start.52 = (f32[1280]{0:T(1024)S(1)}, f32[1280]{0:T(1024)}, u32[]{:S(2)}) copy-start(f32[1280]{0:T(1024)} %param.33) | copy-start | bytes 15364
  378.0 410.5 %all-reduce.15.cloned.1.call-start = ((), (), s32[]{:S(2)}) async-start(), calls=%async_computation.21 | async-start | bytes 10485760 | tf_op jit(solution)/shard_map/psum | solution.py:179
  569.0 5.7 slice-start
  570.0 4.8 slice-start.1
  574.8 6.3 slice-start.4
  581.0 9.6 copy-start.32
  581.1 9.6 copy-start.67
  600.5 319.1 %reduce-scatter.33.cloned.1.call-start = ((), (), s32[]{:S(2)}) async-start(), calls=%async_computation.22 | async-start | bytes 983040 | tf_op jit(solution)/shard_map/reduce_scatter | solution.py:207
  788.5 9.5 copy-start.6
  798.0 11.7 slice-start.2
  798.0 11.7 slice-start.3
  885.3 36.2 %reduce-scatter.35.cloned.1.call-start = ((), (), s32[]{:S(2)}) async-start(), calls=%async_computation.23 | async-start | bytes 983040 | tf_op jit(solution)/shard_map/reduce_scatter | solution.py:213
  887.4 6.4 copy-start.33
  887.4 58.2 %reduce-scatter.61.cloned.1.call-start = ((), (), s32[]{:S(2)}) async-start(), calls=%async_computation.37 | async-start | bytes 1228800
  893.7 93.0 %reduce-scatter.45.cloned.1.call-start = ((), (), s32[]{:S(2)}) async-start(), calls=%async_computation.29 | async-start | bytes 4096000 | tf_op jit(solution)/shard_map/reduce_scatter | solution.py:261
  900.6 127.1 %reduce-scatter.37.cloned.1.call-start = ((), (), s32[]{:S(2)}) async-start(), calls=%async_computation.25 | async-start | bytes 4096000 | tf_op jit(solution)/shard_map/reduce_scatter | solution.py:255
  909.1 159.6 %reduce-scatter.41.cloned.1.call-start = ((), (), s32[]{:S(2)}) async-start(), calls=%async_computation.27 | async-start | bytes 4096000 | tf_op jit(solution)/shard_map/reduce_scatter | solution.py:258
  916.7 179.5 %reduce-scatter.57.cloned.1.call-start = ((), (), s32[]{:S(2)}) async-start(), calls=%async_computation.35 | async-start | bytes 1228800
  921.5 6.4 copy-start.8
  921.5 6.4 copy-start.10
  921.5 6.4 copy-start.12
  921.5 6.4 copy-start.14
  921.6 6.4 copy-start.44
  921.6 6.4 copy-start.46
  921.6 6.4 copy-start.56
  927.8 195.8 %reduce-scatter.53.cloned.1.call-start = ((), (), s32[]{:S(2)}) async-start(), calls=%async_computation.33 | async-start | bytes 1228800
  937.8 213.3 %reduce-scatter.49.cloned.1.call-start = ((), (), s32[]{:S(2)}) async-start(), calls=%async_computation.31 | async-start | bytes 1228800
  942.3 181.5 %copy-start.27 = (bf16[1280,320]{1,0:T(8,128)(2,1)S(1)}, bf16[1280,320]{1,0:T(8,128)(2,1)}, u32[]{:S(2)}) copy-start(bf16[1280,320]{1,0:T(8,128)(2,1)} %copy-done.26) | copy-start | bytes 2457604
  944.6 240.3 %reduce-scatter.63.cloned.1.call-start = ((), (), s32[]{:S(2)}) async-start(), calls=%async_computation.38 | async-start | bytes 368640
  945.7 245.9 %reduce-scatter.47.cloned.1.call-start = ((), (), s32[]{:S(2)}) async-start(), calls=%async_computation.30 | async-start | bytes 1228800 | tf_op jit(solution)/shard_map/reduce_scatter | solution.py:284
  986.7 225.8 %reduce-scatter.39.cloned.1.call-start = ((), (), s32[]{:S(2)}) async-start(), calls=%async_computation.26 | async-start | bytes 1228800 | tf_op jit(solution)/shard_map/reduce_scatter | solution.py:278
  1027.7 206.8 %reduce-scatter.43.cloned.1.call-start = ((), (), s32[]{:S(2)}) async-start(), calls=%async_computation.28 | async-start | bytes 1228800 | tf_op jit(solution)/shard_map/reduce_scatter | solution.py:281
  1068.7 181.4 %reduce-scatter.59.cloned.1.call-start = ((), (), s32[]{:S(2)}) async-start(), calls=%async_computation.36 | async-start | bytes 368640 | tf_op jit(solution)/shard_map/reduce_scatter | solution.py:272
  1096.3 169.3 %reduce-scatter.55.cloned.1.call-start = ((), (), s32[]{:S(2)}) async-start(), calls=%async_computation.34 | async-start | bytes 368640 | tf_op jit(solution)/shard_map/reduce_scatter | solution.py:269
  1123.7 155.5 %reduce-scatter.51.cloned.1.call-start = ((), (), s32[]{:S(2)}) async-start(), calls=%async_computation.32 | async-start | bytes 368640 | tf_op jit(solution)/shard_map/reduce_scatter | solution.py:266
  1127.7 23.6 %copy-start.23 = (bf16[1280,320]{1,0:T(8,128)(2,1)S(1)}, bf16[1280,320]{1,0:T(8,128)(2,1)}, u32[]{:S(2)}) copy-start(bf16[1280,320]{1,0:T(8,128)(2,1)} %copy-done.22) | copy-start | bytes 2457604
  1127.7 23.6 %copy-start.38 = (bf16[512,5,64]{0,2,1:T(8,128)(2,1)S(1)}, bf16[512,5,64]{0,2,1:T(8,128)(2,1)}, u32[]{:S(2)}) copy-start(bf16[512,5,64]{0,2,1:T(8,128)(2,1)} %slice.82) | copy-start | bytes 983044
  1127.7 23.6 %copy-start.47 = (bf16[512,320]{0,1:T(8,128)(2,1)S(1)}, bf16[512,320]{0,1:T(8,128)(2,1)}, u32[]{:S(2)}) copy-start(bf16[512,320]{0,1:T(8,128)(2,1)} %reduce-scatter.35.cloned.1.call-done) | copy-start | bytes 983044
  1151.2 7.3 copy-start.57
  1151.2 7.3 copy-start.58
  1151.2 7.3 copy-start.61
  1151.2 7.3 copy-start.62
  1151.2 134.5 %all-reduce.17.cloned.1.call-start = ((), (), s32[]{:S(2)}) async-start(), calls=%async_computation.24 | async-start | bytes 5242880 | tf_op jit(solution)/shard_map/psum | solution.py:239
  1227.3 58.4 %copy-start.54 = (f32[1280]{0:T(1024)S(1)}, f32[1280]{0:T(1024)}, u32[]{:S(2)}) copy-start(f32[1280]{0:T(1024)} %param.32) | copy-start | bytes 15364
  (42 other events, 101.9 us)
Sparse Core Ops, SparseCore 0:
  154.4 189.7 all-reduce.10
  378.1 187.8 all-reduce.12
  600.6 187.8 all-reduce.14
  1158.6 104.0 all-reduce.16
Sparse Core Ops, SparseCore 1:
  156.3 29.9 all-gather.5
  187.7 29.1 all-gather.3
  218.3 29.1 all-gather.7
  885.4 14.9 reduce-scatter.32
  902.6 16.0 reduce-scatter.34
  921.3 24.3 reduce-scatter.60
  948.1 38.5 reduce-scatter.44
  989.1 38.5 reduce-scatter.36
  1030.1 38.5 reduce-scatter.40
  1071.9 24.3 reduce-scatter.56
  1099.3 24.3 reduce-scatter.52
  1126.8 24.3 reduce-scatter.48
  1153.3 11.8 reduce-scatter.62
  1167.4 18.7 reduce-scatter.46
  1188.4 24.0 reduce-scatter.38
  1214.7 19.7 reduce-scatter.42
  1236.8 13.3 reduce-scatter.58
  1252.4 13.1 reduce-scatter.54
  1267.6 11.5 reduce-scatter.50
where the time goes:
time: 1310 us; the launch traced here: 1300 us
  waiting for transfers between devices  788 us (60%)
  matrix products  205 us (16%)
  blocking collectives  158 us (12%)
  other arithmetic  74.7 us (6%)
  local copies, waits for them, and re-layouts  54.5 us (4%)
  between operations  17.3 us (1%)
    psum x1, waiting for transfers between devices, on_device(): attn_out = lax.psum(attn_terms, 'tensor')  188 us
    psum x1, waiting for transfers between devices, on_device(): grad_after = grad_after + lax.psum(input_terms, 'tensor')  188 us
    psum x1, waiting for transfers between devices, on_device(): merged = lax.psum(merged_terms, 'tensor')  188 us
    unnamed x28, waiting for transfers between devices  77.3 us
    dot_general x17, matrix products, outer_sum(): lax.dot_general(left, right, (((0,), (0,)), ((), ())), preferred_element_...  51.7 us
    reduce_scatter x1, waiting for transfers between devices, on_device(): lax.psum_scatter(grad_gate.astype(jnp.bfloat16), 'shards', scatter_dimens...  40.9 us
    reduce_scatter x1, waiting for transfers between devices, on_device(): lax.psum_scatter(grad_down.astype(jnp.bfloat16), 'shards', scatter_dimens...  40.9 us
    reduce_scatter x1, waiting for transfers between devices, on_device(): lax.psum_scatter(grad_up.astype(jnp.bfloat16), 'shards', scatter_dimensio...  40.9 us
  transfers between devices with their start and end apart: 23, of which 15 were waited for; matrix products, arithmetic and copies ran while one was open for 8% of the time, Pallas kernels for 0%

commit v1 on v0

--- a/solution.py
+++ b/solution.py
@@ -1,3 +1,4 @@
+import functools
 import math
 import jax
 import jax.numpy as jnp
@@ -9,6 +10,13 @@
 CONT_LEN = 256
 EPSILON = 1e-06
 MASKED = -1e30
+
+
+def supply_all_shelves(v0, a_name):
+    return jax.lax.all_gather(v0, a_name).sum(axis=0)
+
+
+produce_rounds = functools.partial(supply_all_shelves, a_name="tensor")
 
 
 def renorm(vector):
@@ -162,7 +170,7 @@
     inner, swiglu_back = jax.vjp(swiglu, up_proj, gate_proj, scale_up, scale_gate)
     inner_low = inner.astype(jnp.bfloat16)
     merged_terms = jnp.dot(inner_low, full_down, preferred_element_type=jnp.float32)
-    merged = lax.psum(merged_terms, "tensor")
+    merged = produce_rounds(merged_terms)
     block_whole, out_back = jax.vjp(residual_step, after_attn, merged, alpha_mlp)
     block_low = block_whole.astype(jnp.bfloat16)
     grad_after, grad_merged, grad_alpha_mlp = out_back(cotangent.astype(jnp.float32))

time: 1310 us -> 1490 us (1.14)
  waiting for transfers between devices: 788 us -> 956 us
    all_gather x0 -> x1, waiting for transfers between devices: none -> 355 us  [supply_all_shelves(): return jax.lax.all_gather(v0, a_name).sum(axis=0)]
    psum x1 -> x0, waiting for transfers between devices: 188 us -> none  [on_device(): merged = lax.psum(merged_terms, 'tensor')]
  transfers between devices with their start and end apart: 23 -> 23, of which waited for: 15 -> 15; matrix products, arithmetic and copies ran while one was open for 8% -> 7% of each run, Pallas kernels for 0% -> 0%
where the time goes in v1:
time: 1490 us; the launch traced here: 1480 us
  waiting for transfers between devices  956 us (64%)
  matrix products  205 us (14%)
  blocking collectives  157 us (11%)
  other arithmetic  85.4 us (6%)
  local copies, waits for them, and re-layouts  54.6 us (4%)
  between operations  17.2 us (1%)
    all_gather x1, waiting for transfers between devices, supply_all_shelves(): return jax.lax.all_gather(v0, a_name).sum(axis=0)  355 us
    psum x1, waiting for transfers between devices, on_device(): attn_out = lax.psum(attn_terms, 'tensor')  188 us
    psum x1, waiting for transfers between devices, on_device(): grad_after = grad_after + lax.psum(input_terms, 'tensor')  187 us
    unnamed x28, waiting for transfers between devices  77.3 us
    dot_general x17, matrix products, outer_sum(): lax.dot_general(left, right, (((0,), (0,)), ((), ())), preferred_element_...  51.7 us
    reduce_scatter x1, waiting for transfers between devices, on_device(): lax.psum_scatter(grad_gate.astype(jnp.bfloat16), 'shards', scatter_dimens...  41 us
    reduce_scatter x1, waiting for transfers between devices, on_device(): lax.psum_scatter(grad_down.astype(jnp.bfloat16), 'shards', scatter_dimens...  40.9 us
    reduce_scatter x1, waiting for transfers between devices, on_device(): lax.psum_scatter(grad_up.astype(jnp.bfloat16), 'shards', scatter_dimensio...  40.9 us
  transfers between devices with their start and end apart: 23, of which 15 were waited for; matrix products, arithmetic and copies ran while one was open for 7% of the time, Pallas kernels for 0%

profile of v1, /device:TPU:0, one launch (start us, length us, event | category | flops | bytes accessed | tf_op | source)
XLA Modules:
  0.0 1477.5 jit_solution(2544227415093545300)
XLA Ops:
  11.3 11.3 all_gather.54
  22.7 10.1 all_gather.55
  32.8 3.2 fusion.70
  40.0 10.6 all_gather.56
  55.9 9.5 all_gather.57
  66.5 10.8 all_gather.58
  81.6 57.1 %while.28 = (s32[]{:T(128)}, bf16[5,1024,64]{1,2,0:T(8,128)(2,1)S(1)}, f32[5,1024]{1,0:T(8,128)S(1)}, bf16[5,1024,64]{2,1,0:T(8,128)(2,1)}, bf16[5,1536,64]{2,1,...) while((s32[]{:T(128)}, ...), condition=%wide.region_5.6_spmd.clone, body=%wide.region_2.5_spmd.clone.sunk | while | flops 421592064 | bytes 45289628 | solution.py:162
  81.6 3.4 fusion.135
  88.8 4.2 fusion.137
  93.0 3.4 fusion.135
  100.2 4.2 fusion.137
  104.5 3.4 fusion.135
  111.7 4.2 fusion.137
  115.9 3.4 fusion.135
  123.1 4.2 fusion.137
  127.3 3.4 fusion.135
  134.5 4.2 fusion.137
  140.1 9.3 all_gather.59
  150.4 3.9 fusion.72
  156.1 188.1 %all-reduce.10.cloned.1.call-done = f32[1024,1280]{1,0:T(8,128)} async-done(((f32[1024,1280]{1,0:T(8,128)}), f32[1024,1280]{1,0:T(8,128)}) %all-reduce.10.cloned.1.call-update) | async-done | bytes 5242896 | tf_op jit(solution)/shard_map/psum | solution.py:165
  352.5 8.1 fusion.73
  360.7 8.7 multiply_convert_fusion.4
  369.3 8.7 fusion.74
  378.5 355.5 %all-gather.12.cloned.1.call-done = f32[4096,1280]{1,0:T(8,128)} async-done(((f32[1024,1280]{1,0:T(8,128)}), f32[4096,1280]{1,0:T(8,128)}) %all-gather.12.cloned.1.call-update) | async-done | bytes 20971536 | tf_op jit(solution)/shard_map/all_gather | solution.py:16
  734.0 11.0 reduce_sum.192
  749.0 4.4 fusion.49
  759.8 9.5 multiply_reduce_fusion.1
  769.4 3.6 fusion.75
  773.7 5.5 convolution_add_fusion
  779.5 187.4 %all-reduce.12.cloned.1.call-done = f32[1024,1280]{1,0:T(8,128)} async-done(((f32[1024,1280]{1,0:T(8,128)}), f32[1024,1280]{1,0:T(8,128)}) %all-reduce.12.cloned.1.call-update) | async-done | bytes 5242896 | tf_op jit(solution)/shard_map/psum | solution.py:187
  966.8 9.5 multiply_reduce_fusion.3
  976.4 11.6 multiply_reduce_fusion.4
  992.7 68.5 %while.29 = (s32[]{:T(128)}, f32[5,1024,64]{1,2,0:T(8,128)}, f32[5,1536,64]{1,2,0:T(8,128)}, bf16[5,1536,64]{1,2,0:T(8,128)(2,1)}, bf16[5,1024,64]{2,1,0:T(8,128...) while((s32[]{:T(128)}, f32[5,1024,64]{1,2,0:T(8,128)}, ...), condition=%wide.region_19.20_spmd.clone, body=%wide.region_17.19_spmd.clone.sunk | while | flops 1027243008 | bytes 50515088 | solution.py:209
  994.8 4.5 multiply_reduce_fusion.18
  1008.5 4.5 multiply_reduce_fusion.18
  1022.2 4.5 multiply_reduce_fusion.18
  1035.9 4.5 multiply_reduce_fusion.18
  1049.5 4.5 multiply_reduce_fusion.18
  1065.9 3.8 convolution_convert_fusion.3
  1072.0 6.8 convolution_convert_fusion
  1080.6 6.7 convolution_convert_fusion.2
  1087.4 7.5 convolution_convert_fusion.1
  1099.8 4.0 fusion.57
  1124.0 40.9 %reduce-scatter.45.cloned.1.call-done = bf16[1280,320]{0,1:T(8,128)(2,1)} async-done(((bf16[1280,1280]{0,1:T(8,128)(2,1)}), bf16[1280,320]{0,1:T(8,128)(2,1)}) %reduce-scatter.45.cloned.1.call-update) | async-done | bytes 819216 | tf_op jit(solution)/shard_map/reduce_scatter | solution.py:269
  1165.0 40.9 %reduce-scatter.37.cloned.1.call-done = bf16[320,1280]{1,0:T(8,128)(2,1)} async-done(((bf16[1280,1280]{1,0:T(8,128)(2,1)}), bf16[320,1280]{1,0:T(8,128)(2,1)}) %reduce-scatter.37.cloned.1.call-update) | async-done | bytes 819216 | tf_op jit(solution)/shard_map/reduce_scatter | solution.py:263
  1206.0 41.0 %reduce-scatter.41.cloned.1.call-done = bf16[320,1280]{1,0:T(8,128)(2,1)} async-done(((bf16[1280,1280]{1,0:T(8,128)(2,1)}), bf16[320,1280]{1,0:T(8,128)(2,1)}) %reduce-scatter.41.cloned.1.call-update) | async-done | bytes 819216 | tf_op jit(solution)/shard_map/reduce_scatter | solution.py:266
  1247.0 27.5 %reduce-scatter.57.cloned.1.call-done = bf16[320,320]{1,0:T(8,128)(2,1)} async-done(((bf16[1280,320]{1,0:T(8,128)(2,1)}), bf16[320,320]{1,0:T(8,128)(2,1)}) %reduce-scatter.57.cloned.1.call-update) | async-done | bytes 204816
  1274.5 27.3 %reduce-scatter.53.cloned.1.call-done = bf16[320,320]{1,0:T(8,128)(2,1)} async-done(((bf16[1280,320]{1,0:T(8,128)(2,1)}), bf16[320,320]{1,0:T(8,128)(2,1)}) %reduce-scatter.53.cloned.1.call-update) | async-done | bytes 204816
  1302.0 3.9 fusion.77
  1305.9 3.8 fusion.76
  1309.8 19.6 %reduce-scatter.49.cloned.1.call-done = bf16[320,320]{1,0:T(8,128)(2,1)} async-done(((bf16[1280,320]{1,0:T(8,128)(2,1)}), bf16[320,320]{1,0:T(8,128)(2,1)}) %reduce-scatter.49.cloned.1.call-update) | async-done | bytes 204816
  1329.5 7.1 add_convert_fusion.1
  1336.8 26.4 %all-reduce.5 = (f32[320]{0:T(512)}, f32[1280]{0:T(1024)}, f32[1280]{0:T(1024)}, f32[1280]{0:T(1024)}, f32[1280]{0:T(1024)}) all-reduce(f32[320]{0:T(512)S(1)} %add.194, f32[1280]{0:T(1024)S(1)} %copy-done.58, f32[1280]{0:T(1024)S(1)} %copy-done.57, ...), channel_id=1, replica_groups=mesh['shards'=4,'context'=2,'tensor'=4] {'shards','context'}, use_global_device_ids=true, to_apply=%region_41.42 | all-reduce | flops 5440 | bytes 43520 | tf_op jit(solution)/shard_map/psum | solution.py:319
  1363.2 5.7 all_gather.68
  1369.9 19.3 %all_gather.71 = bf16[1280,320]{0,1:T(8,128)(2,1)S(1)} all-gather(bf16[1280,160]{0,1:T(8,128)(2,1)} %reduce-scatter.47.cloned.1.call-done), channel_id=1, replica_groups=mesh['shards'=4,'context'=2,'tensor'=4] {'context'}, dimensions={1}, use_global_device_ids=true | all-gather | bytes 1228800 | tf_op jit(solution)/shard_map/all_gather | solution.py:315
  1390.7 13.3 all_gather.69
  1405.3 7.4 reduce-scatter.43.cloned.1.call-done
  1412.7 13.4 all_gather.70
  1428.4 5.9 all_gather.67
  1435.2 8.6 reduce-scatter.55.cloned.1.call-done
  1443.7 5.7 all_gather.66
  1450.3 7.1 reduce-scatter.51.cloned.1.call-done
  1457.4 5.7 all_gather.65
  1463.9 5.7 add_convert_fusion
  (344 shorter events, 153.9 us)
Async XLA Ops:
  8.0 336.2 %all-reduce.10.cloned.1.call-start = ((), (), s32[]{:S(2)}) async-start(), calls=%async_computation.16 | async-start | bytes 10485760 | tf_op jit(solution)/shard_map/psum | solution.py:165
  22.7 13.3 copy-start.24
  22.7 13.3 copy-start.15
  38.5 13.1 copy-start.43
  39.5 12.1 copy-start.45
  39.6 12.1 copy-start.55
  51.6 13.7 copy-start.16
  66.5 15.1 %copy-start.35 = (bf16[5,1024,64]{1,2,0:T(8,128)(2,1)S(1)}, bf16[5,1024,64]{1,2,0:T(8,128)(2,1)}, u32[]{:S(2)}) copy-start(bf16[5,1024,64]{1,2,0:T(8,128)(2,1)} %custom-call) | copy-start | bytes 1966084
  66.5 15.1 %copy-start.59 = (s32[1024]{0:T(1024)S(1)}, s32[1024]{0:T(1024)}, u32[]{:S(2)}) copy-start(s32[1024]{0:T(1024)} %param.23) | copy-start | bytes 12292
  66.5 15.1 %copy-start.64 = (s32[1024]{0:T(1024)S(1)}, s32[1024]{0:T(1024)}, u32[]{:S(2)}) copy-start(s32[1024]{0:T(1024)} %param.22) | copy-start | bytes 12292
  138.7 15.6 %copy-start.36 = (bf16[5,1024,64]{1,2,0:T(8,128)(2,1)}, bf16[5,1024,64]{1,2,0:T(8,128)(2,1)S(1)}, u32[]{:S(2)}) copy-start(bf16[5,1024,64]{1,2,0:T(8,128)(2,1)S(1)} %get-tuple-element.106) | copy-start | bytes 1966084
  154.3 198.2 %all-gather.8.cloned.1.call-start = ((), (), s32[]{:S(2)}) async-start(), calls=%async_computation.18 | async-start | bytes 4096000 | tf_op jit(solution)/shard_map/all_gather | solution.py:103
  154.9 192.4 %copy-start.53 = (f32[1280]{0:T(1024)S(1)}, f32[1280]{0:T(1024)}, u32[]{:S(2)}) copy-start(f32[1280]{0:T(1024)} %param.32) | copy-start | bytes 15364
  154.9 205.7 %all-gather.6.cloned.1.call-start = ((), (), s32[]{:S(2)}) async-start(), calls=%async_computation.17 | async-start | bytes 4096000 | tf_op jit(solution)/shard_map/all_gather | solution.py:102
  155.5 213.8 %all-gather.10.cloned.1.call-start = ((), (), s32[]{:S(2)}) async-start(), calls=%async_computation.19 | async-start | bytes 4096000 | tf_op jit(solution)/shard_map/all_gather | solution.py:104
  156.1 577.9 %all-gather.12.cloned.1.call-start = ((), (), s32[]{:S(2)}) async-start(), calls=%async_computation.30 | async-start | bytes 26214400 | tf_op jit(solution)/shard_map/all_gather | solution.py:16
  352.5 8.2 copy-start.30
  352.5 8.2 copy-start.69
  352.5 8.2 copy-start.70
  378.0 588.8 %all-reduce.12.cloned.1.call-start = ((), (), s32[]{:S(2)}) async-start(), calls=%async_computation.20 | async-start | bytes 10485760 | tf_op jit(solution)/shard_map/psum | solution.py:187
  734.0 14.1 copy-start.4
  748.0 5.4 slice-start
  749.0 4.5 slice-start.1
  753.5 6.3 slice-start.4
  759.7 9.6 copy-start.32
  759.8 9.6 copy-start.67
  779.2 318.7 %reduce-scatter.33.cloned.1.call-start = ((), (), s32[]{:S(2)}) async-start(), calls=%async_computation.21 | async-start | bytes 983040 | tf_op jit(solution)/shard_map/reduce_scatter | solution.py:215
  966.8 9.5 copy-start.6
  976.3 11.7 slice-start.2
  976.3 11.7 slice-start.3
  1061.2 4.7 copy-start.37
  1063.6 36.2 %reduce-scatter.35.cloned.1.call-start = ((), (), s32[]{:S(2)}) async-start(), calls=%async_computation.22 | async-start | bytes 983040 | tf_op jit(solution)/shard_map/reduce_scatter | solution.py:221
  1065.7 6.3 copy-start.33
  1065.7 58.2 %reduce-scatter.61.cloned.1.call-start = ((), (), s32[]{:S(2)}) async-start(), calls=%async_computation.37 | async-start | bytes 1228800
  1072.0 93.0 %reduce-scatter.45.cloned.1.call-start = ((), (), s32[]{:S(2)}) async-start(), calls=%async_computation.28 | async-start | bytes 4096000 | tf_op jit(solution)/shard_map/reduce_scatter | solution.py:269
  1078.9 127.0 %reduce-scatter.37.cloned.1.call-start = ((), (), s32[]{:S(2)}) async-start(), calls=%async_computation.24 | async-start | bytes 4096000 | tf_op jit(solution)/shard_map/reduce_scatter | solution.py:263
  1087.3 159.6 %reduce-scatter.41.cloned.1.call-start = ((), (), s32[]{:S(2)}) async-start(), calls=%async_computation.26 | async-start | bytes 4096000 | tf_op jit(solution)/shard_map/reduce_scatter | solution.py:266
  1095.0 179.5 %reduce-scatter.57.cloned.1.call-start = ((), (), s32[]{:S(2)}) async-start(), calls=%async_computation.35 | async-start | bytes 1228800
  1099.8 6.4 copy-start.8
  1099.8 6.4 copy-start.10
  1099.8 6.4 copy-start.12
  1099.8 6.4 copy-start.14
  1099.8 6.4 copy-start.44
  1099.8 6.4 copy-start.46
  1099.8 6.4 copy-start.56
  1106.1 195.8 %reduce-scatter.53.cloned.1.call-start = ((), (), s32[]{:S(2)}) async-start(), calls=%async_computation.33 | async-start | bytes 1228800
  1116.1 213.3 %reduce-scatter.49.cloned.1.call-start = ((), (), s32[]{:S(2)}) async-start(), calls=%async_computation.31 | async-start | bytes 1228800
  1120.5 181.4 %copy-start.27 = (bf16[1280,320]{1,0:T(8,128)(2,1)S(1)}, bf16[1280,320]{1,0:T(8,128)(2,1)}, u32[]{:S(2)}) copy-start(bf16[1280,320]{1,0:T(8,128)(2,1)} %copy-done.26) | copy-start | bytes 2457604
  1122.8 240.3 %reduce-scatter.63.cloned.1.call-start = ((), (), s32[]{:S(2)}) async-start(), calls=%async_computation.38 | async-start | bytes 368640
  1123.9 245.9 %reduce-scatter.47.cloned.1.call-start = ((), (), s32[]{:S(2)}) async-start(), calls=%async_computation.29 | async-start | bytes 1228800 | tf_op jit(solution)/shard_map/reduce_scatter | solution.py:292
  1164.9 225.8 %reduce-scatter.39.cloned.1.call-start = ((), (), s32[]{:S(2)}) async-start(), calls=%async_computation.25 | async-start | bytes 1228800 | tf_op jit(solution)/shard_map/reduce_scatter | solution.py:286
  1205.9 206.8 %reduce-scatter.43.cloned.1.call-start = ((), (), s32[]{:S(2)}) async-start(), calls=%async_computation.27 | async-start | bytes 1228800 | tf_op jit(solution)/shard_map/reduce_scatter | solution.py:289
  1247.0 181.4 %reduce-scatter.59.cloned.1.call-start = ((), (), s32[]{:S(2)}) async-start(), calls=%async_computation.36 | async-start | bytes 368640 | tf_op jit(solution)/shard_map/reduce_scatter | solution.py:280
  1274.5 169.3 %reduce-scatter.55.cloned.1.call-start = ((), (), s32[]{:S(2)}) async-start(), calls=%async_computation.34 | async-start | bytes 368640 | tf_op jit(solution)/shard_map/reduce_scatter | solution.py:277
  1301.9 155.5 %reduce-scatter.51.cloned.1.call-start = ((), (), s32[]{:S(2)}) async-start(), calls=%async_computation.32 | async-start | bytes 368640 | tf_op jit(solution)/shard_map/reduce_scatter | solution.py:274
  1305.9 23.6 %copy-start.23 = (bf16[1280,320]{1,0:T(8,128)(2,1)S(1)}, bf16[1280,320]{1,0:T(8,128)(2,1)}, u32[]{:S(2)}) copy-start(bf16[1280,320]{1,0:T(8,128)(2,1)} %copy-done.22) | copy-start | bytes 2457604
  1305.9 23.6 %copy-start.38 = (bf16[512,5,64]{0,2,1:T(8,128)(2,1)S(1)}, bf16[512,5,64]{0,2,1:T(8,128)(2,1)}, u32[]{:S(2)}) copy-start(bf16[512,5,64]{0,2,1:T(8,128)(2,1)} %slice.82) | copy-start | bytes 983044
  1305.9 23.6 %copy-start.47 = (bf16[512,320]{0,1:T(8,128)(2,1)S(1)}, bf16[512,320]{0,1:T(8,128)(2,1)}, u32[]{:S(2)}) copy-start(bf16[512,320]{0,1:T(8,128)(2,1)} %reduce-scatter.35.cloned.1.call-done) | copy-start | bytes 983044
  1329.4 7.3 copy-start.57
  1329.4 7.3 copy-start.58
  1329.4 7.3 copy-start.61
  1329.4 7.3 copy-start.62
  1329.5 134.5 %all-reduce.14.cloned.1.call-start = ((), (), s32[]{:S(2)}) async-start(), calls=%async_computation.23 | async-start | bytes 5242880 | tf_op jit(solution)/shard_map/psum | solution.py:247
  1405.3 58.6 %copy-start.54 = (f32[1280]{0:T(1024)S(1)}, f32[1280]{0:T(1024)}, u32[]{:S(2)}) copy-start(f32[1280]{0:T(1024)} %param.32) | copy-start | bytes 15364
  (42 other events, 101.5 us)
Sparse Core Ops, SparseCore 0:
  154.4 189.7 all-reduce.9
  378.2 355.7 all-gather.11
  779.3 187.4 all-reduce.11
  1336.8 104.0 all-reduce.13
Sparse Core Ops, SparseCore 1:
  156.4 29.9 all-gather.7
  187.8 29.1 all-gather.5
  218.4 29.1 all-gather.9
  1063.7 14.9 reduce-scatter.32
  1080.9 16.0 reduce-scatter.34
  1099.5 24.3 reduce-scatter.60
  1126.3 38.5 reduce-scatter.44
  1167.3 38.5 reduce-scatter.36
  1208.3 38.5 reduce-scatter.40
  1250.1 24.3 reduce-scatter.56
  1277.5 24.3 reduce-scatter.52
  1305.0 24.3 reduce-scatter.48
  1331.5 11.8 reduce-scatter.62
  1345.7 18.7 reduce-scatter.46
  1366.7 24.0 reduce-scatter.38
  1393.0 19.7 reduce-scatter.42
  1415.0 13.4 reduce-scatter.58
  1430.7 13.0 reduce-scatter.54
  1445.9 11.5 reduce-scatter.50
